TPU v7x, 256 devices: a whole 4x4x8 slice. The times are simulated.
256 devices in a mesh: lat: 4 (over x_lo, core), lon: 64 (over x_hi, z, y).
Axes of the slice: x: 4 (x_hi: 2, x_lo: 2; x = x_hi * 2 + x_lo), y: 4, z: 8, core: 2. Of those that a mesh axis runs over, the one named last changes fastest.
Arguments:
- adjoint_in: float32 [16, 3, 136, 8192], P('lat', None, None, 'lon'), may hold values from -6 to 6
- frac_x: float32 [16, 8192], P('lat', 'lon'), may hold values from 0 to 1
- frac_y: float32 [16, 8192], P('lat', 'lon'), may hold values from 0 to 1
- dep_tile: int32 [16], P('lat'), may hold values from -1 to 0, as said below
- dep_col: int32 [16], P('lat'), may hold values from 0 to 127
- block_inverse: float32 [16, 2, 68, 68], P('lat'), may hold values from -0.25 to 1
- coupling: float32 [16, 8192], P('lat', 'lon'), may hold values from 0.15 to 0.6
Outputs:
- adjoint_out: float32 [16, 3, 136, 8192], P('lat', None, None, 'lon')
Inputs may be any that keep to these rules, and one draw needn't show every extreme that they name: dep_tile * 128 + dep_col is the row's departure offset in columns; it equals -128 in some row and 127 in another.
All inputs are finite; a program needn't handle non-finite values.
Results may differ from a plain program's by a relative error of at most 0.0003.
Values sent between devices are 32-bit elements; how exact they have to be, the bound alone decides.
A program may use at most 64 MiB of HBM per device.

v0:
```python
import jax
import jax.numpy as jnp
from jax import lax
from jax.sharding import PartitionSpec as P

REACH = 1


def passed_along(x, axis, by):
    devices = lax.axis_size(axis)
    return lax.ppermute(x, axis, [(i, (i + by) % devices) for i in range(devices)])


def shifted(x, axis, by):
    devices = lax.axis_size(axis)
    pairs = [(i, i + by) for i in range(devices) if 0 <= i + by < devices]
    return lax.ppermute(x, axis, pairs)


def cubic_weights(fraction):
    plus_one = fraction + 1.0
    minus_one = fraction - 1.0
    minus_two = fraction - 2.0
    return jnp.stack(
        [
            -fraction * minus_one * minus_two / 6.0,
            plus_one * minus_one * minus_two / 2.0,
            -plus_one * fraction * minus_two / 2.0,
            plus_one * fraction * minus_one / 6.0,
        ]
    )


def vertical(field_in, inverse, coupling):
    row_count, tracer_count, level_count, col_count = field_in.shape
    block_count = inverse.shape[1]
    block_size = inverse.shape[2]
    blocks = field_in.reshape(row_count, tracer_count, block_count, block_size, col_count)
    first_sweep = jnp.einsum("rnij,rtnjc->rtnic", inverse, blocks, precision=lax.Precision.HIGHEST)
    coupling_now = coupling[:, None, None, :]
    adjusted = blocks.at[:, :, :-1, block_size - 1, :].add(
        coupling_now * first_sweep[:, :, 1:, 0, :]
    )
    adjusted = adjusted.at[:, :, 1:, 0, :].add(
        coupling_now * first_sweep[:, :, :-1, block_size - 1, :]
    )
    second_sweep = jnp.einsum(
        "rnij,rtnjc->rtnic", inverse, adjusted, precision=lax.Precision.HIGHEST
    )
    return second_sweep.reshape(row_count, tracer_count, level_count, col_count)


def prepare(values, frac_x, frac_y):
    weights_x = jnp.swapaxes(cubic_weights(frac_x), 0, 1)
    weights_y = jnp.swapaxes(cubic_weights(frac_y), 0, 1)
    paired = weights_y[:, :, None, :] * weights_x[:, None, :, :]
    zero_block = jnp.zeros(values.shape, jnp.float32)
    zero_pairs = jnp.zeros(paired.shape, jnp.float32)
    padded_values = jnp.concatenate([zero_block, values, zero_block], axis=3)
    padded_pairs = jnp.concatenate([zero_pairs, paired, zero_pairs], axis=3)
    return (padded_values, padded_pairs)


def tile_terms(padded_values, padded_pairs, offsets, k, col_count):
    row_count = padded_values.shape[0]

    def one_row(packed):
        row_values, row_pairs, offset = packed
        summed = None
        for b in range(4):
            delta = k * col_count + 1 - b - offset
            reached = (jnp.abs(delta) < col_count).astype(jnp.float32)
            start = jnp.clip(col_count + delta, 0, 2 * col_count)
            sliced = lax.dynamic_slice_in_dim(row_values, start, col_count, 2)
            factor = lax.dynamic_slice_in_dim(row_pairs[:, b, :], start, col_count, 1) * reached
            product_term = factor[:, None, None, :] * sliced[None]
            summed = product_term if b == 0 else summed + product_term
        return summed

    summed = lax.map(one_row, (padded_values, padded_pairs, offsets))
    extended = jnp.zeros((row_count + 3,) + summed.shape[2:], jnp.float32)
    for a in range(4):
        extended = extended.at[a : a + row_count].add(summed[:, a])
    return extended


def on_device(adjoint_in, frac_x, frac_y, dep_tile, dep_col, block_inverse, coupling):
    row_count = adjoint_in.shape[0]
    col_count = adjoint_in.shape[3]
    offsets = dep_tile * col_count + dep_col
    far_tiles = REACH + 1
    padded_values, padded_pairs = prepare(adjoint_in, frac_x, frac_y)
    home_sum = tile_terms(padded_values, padded_pairs, offsets, 0, col_count)
    for k in range(-far_tiles, far_tiles + 1):
        if k != 0:
            outgoing = tile_terms(padded_values, padded_pairs, offsets, k, col_count)
            home_sum = home_sum + passed_along(outgoing, "lon", k)
    upper_rim = shifted(home_sum[row_count + 1 : row_count + 3], "lat", 1)
    lower_rim = shifted(home_sum[0:1], "lat", -1)
    interior = home_sum[1 : row_count + 1]
    interior = interior.at[0:2].add(upper_rim)
    interior = interior.at[row_count - 1 : row_count].add(lower_rim)
    return vertical(interior, block_inverse, coupling)


def solution(mesh):
    return jax.shard_map(
        on_device,
        mesh=mesh,
        in_specs=(
            P("lat", None, None, "lon"),
            P("lat", "lon"),
            P("lat", "lon"),
            P("lat"),
            P("lat"),
            P("lat", None, None, None),
            P("lat", "lon"),
        ),
        out_specs=P("lat", None, None, "lon"),
        check_vma=False,
    )
```

profile of v0, /device:TPU:1, one launch (start us, length us, event | category | flops | bytes accessed | tf_op | source)
XLA Modules:
  0.0 238.5 jit_solution(2708873072605784376)
XLA Ops:
  1.6 1.3 pad_maximum_fusion
  3.0 1.9 broadcast.990.clone2.3
  4.9 29.5 %while.90 = (s32[]{:T(128)}, f32[4,4,3,136,128]{4,3,2,0,1:T(8,128)}, f32[4,4,4,384]{3,1,2,0:T(4,128)S(1)}, s32[4]{0:T(128)S(1)}, f32[4,3,136,384]{3,2,1,0:T(8,12...) while((s32[]{:T(128)}, ...), condition=%wide.region_3.4_spmd, body=%wide.region_2.3_spmd.sunk | while | flops 1464355 | bytes 3466337 | solution.py:80
  11.2 1.1 bitcast_dynamic-update-slice_fusion.9
  33.3 1.1 bitcast_dynamic-update-slice_fusion.9
  34.4 1.4 slice_bitcast_fusion.5
  35.8 1.2 scatter-add.86
  37.0 2.1 fusion.55
  39.1 2.1 fusion.50
  41.3 2.2 fusion.49
  43.5 11.5 %collective-permute-start = (f32[7,3,136,128]{3,2,1,0:T(8,128)}, f32[7,3,136,128]{3,2,1,0:T(8,128)}, u32[]{:S(2)}, u32[]{:S(2)}) collective-permute-start(f32[7,3,136,128]{3,2,1,0:T(8,128)} %fusion.49), channel_id=1, source_target_pairs={{0,62},{1,63},{2,0},{3,1},{4,2},{5,3},{6,4},{7,5},{8,6},{9,7},{10,... | collective-permute-start | bytes 4386824 | tf_op jit(solution)/shard_map/ppermute | solution.py:11
  54.9 1.9 broadcast.990.clone2.1
  56.9 29.1 %while.91 = (s32[]{:T(128)}, f32[4,4,3,136,128]{4,3,2,0,1:T(8,128)}, f32[4,4,4,384]{3,1,2,0:T(4,128)S(1)}, s32[4]{0:T(128)S(1)}, f32[4,3,136,384]{3,2,1,0:T(8,12...) while((s32[]{:T(128)}, ...), condition=%wide.region_5.6_spmd, body=%wide.region_4.5_spmd.sunk | while | flops 1464355 | bytes 3466329 | solution.py:80
  63.0 1.1 bitcast_dynamic-update-slice_fusion.10
  84.9 1.1 bitcast_dynamic-update-slice_fusion.10
  86.0 1.4 slice_bitcast_fusion.4
  87.3 1.2 scatter-add.94
  88.6 2.2 fusion.54
  90.7 2.1 fusion.48
  92.9 2.1 fusion.47
  95.8 1.9 broadcast.990.clone2
  97.7 29.5 %while.92 = (s32[]{:T(128)}, f32[4,4,3,136,128]{4,3,2,0,1:T(8,128)}, f32[4,4,4,384]{3,1,2,0:T(4,128)S(1)}, s32[4]{0:T(128)S(1)}, f32[4,3,136,384]{3,2,1,0:T(8,12...) while((s32[]{:T(128)}, ...), condition=%wide.region_7.8_spmd, body=%wide.region_6.7_spmd.sunk | while | flops 1464355 | bytes 3466321 | solution.py:80
  126.1 1.1 bitcast_dynamic-update-slice_fusion.11
  127.2 1.4 slice_bitcast_fusion.3
  128.5 1.2 scatter-add.100
  129.8 2.1 fusion.53
  131.9 2.1 fusion.46
  134.1 2.1 fusion.45
  136.9 29.2 %while.93 = (s32[]{:T(128)}, f32[4,4,3,136,128]{4,3,2,1,0:T(8,128)}, f32[4,4,4,384]{3,1,2,0:T(4,128)S(1)}, s32[4]{0:T(128)S(1)}, f32[4,3,136,384]{3,2,1,0:T(8,12...) while((s32[]{:T(128)}, ...), condition=%wide.region_9.10_spmd, body=%wide.region_8.9_spmd.sunk | while | flops 1464355 | bytes 3466329 | solution.py:80
  150.4 1.1 add_dynamic-update-slice_fusion.2
  166.1 1.4 slice_bitcast_fusion.2
  167.5 1.2 scatter-add.106
  168.7 2.2 fusion.44
  170.8 2.1 fusion.42
  173.0 2.1 fusion.40
  175.8 1.9 broadcast.990.clone2.2
  177.8 29.5 %while.89 = (s32[]{:T(128)}, f32[4,4,3,136,128]{4,3,2,0,1:T(8,128)}, f32[4,4,4,384]{3,1,2,0:T(4,128)S(1)}, s32[4]{0:T(128)S(1)}, f32[4,3,136,384]{3,2,1,0:T(8,12...) while((s32[]{:T(128)}, ...), condition=%wide.region_1.2_spmd, body=%wide.region_0.1_spmd.sunk | while | flops 1464355 | bytes 3466321 | solution.py:80
  184.0 1.1 bitcast_dynamic-update-slice_fusion.8
  206.1 1.1 bitcast_dynamic-update-slice_fusion.8
  207.2 1.4 slice_bitcast_fusion.6
  210.0 3.5 %collective-permute-done.3 = f32[7,3,136,128]{3,2,1,0:T(8,128)} collective-permute-done((f32[7,3,136,128]{3,2,1,0:T(8,128)}, f32[7,3,136,128]{3,2,1,0:T(8,128)}, u32[]{:S(2)}, u32[]{:S(2)}) %collective-permute-start.3) | collective-permute-done | bytes 1462304 | tf_op jit(solution)/shard_map/ppermute | solution.py:11
  213.5 3.0 %add_add_fusion = f32[7,3,136,128]{3,2,1,0:T(8,128)S(1)} fusion(f32[7,3,136,128]{3,2,1,0:T(8,128)} %collective-permute-done.3, f32[7,3,136,128]{3,2,1,0:T(8,128)} %collective-permute-done.2, f32[7,3,136,128]{3,2,1,0:T(8,128)} %collective-permute-done.1, f32[7,3,136,128]{3,2,1,0:T(8,128)S(1)} %fusion.51, f32[7,3,136,128]{3,2,1,0:T(8,128)} %collective-permute-done), kind=kLoop, calls=%fused_computation.91 | loop fusion | flops 1462272 | bytes 8773632 | tf_op jit(solution)/shard_map/add | solution.py:97
  216.6 4.5 %collective-permute-start.4 = (f32[2,3,136,128]{3,2,1,0:T(8,128)S(1)}, f32[2,3,136,128]{3,2,1,0:T(8,128)S(1)}, u32[]{:S(2)}, u32[]{:S(2)}) collective-permute-start(f32[2,3,136,128]{3,2,1,0:T(8,128)S(1)} %slice.996), channel_id=1, source_target_pairs={{0,64},{64,128},{128,192},{1,65},{65,129},{129,193},{2,66},{66,130... | collective-permute-start | bytes 1253384 | tf_op jit(solution)/shard_map/ppermute | solution.py:17
  222.5 2.1 collective-permute-start.5
  224.6 1.4 collective-permute-done.4
  226.1 3.6 %collective-permute-done.5 = f32[1,3,136,128]{3,2,1,0:T(8,128)S(1)} collective-permute-done((f32[1,3,136,128]{3,2,1,0:T(8,128)S(1)}, f32[1,3,136,128]{3,2,1,0:T(8,128)S(1)}, u32[]{:S(2)}, u32[]{:S(2)}) %collective-permute-start.5) | collective-permute-done | bytes 208928 | tf_op jit(solution)/shard_map/ppermute | solution.py:17
  232.0 1.9 broadcast_select_fusion
  234.0 1.3 scatter-add.116
  (192 shorter events, 47.7 us)
Async XLA Ops:
  0.0 230.0 %copy-start = (f32[4,2,68,68]{3,1,2,0:T(2,128)S(1)}, f32[4,2,68,68]{3,1,2,0:T(2,128)}, u32[]{:S(2)}) copy-start(f32[4,2,68,68]{3,1,2,0:T(2,128)} %param.70) | copy-start | bytes 443908
  1.5 1.4 copy-start.9
  1.5 1.4 copy-start.10
  34.4 2.6 %copy-start.1 = (f32[4,4,3,136,128]{4,3,2,0,1:T(8,128)S(1)}, f32[4,4,3,136,128]{4,3,2,0,1:T(8,128)}, u32[]{:S(2)}) copy-start(f32[4,4,3,136,128]{4,3,2,0,1:T(8,128)} %get-tuple-element.784) | copy-start | bytes 10027012
  43.5 166.5 %collective-permute-start = (f32[7,3,136,128]{3,2,1,0:T(8,128)}, f32[7,3,136,128]{3,2,1,0:T(8,128)}, u32[]{:S(2)}, u32[]{:S(2)}) collective-permute-start(f32[7,3,136,128]{3,2,1,0:T(8,128)} %fusion.49), channel_id=1, source_target_pairs={{0,62},{1,63},{2,0},{3,1},{4,2},{5,3},{6,4},{7,5},{8,6},{9,7},{10,... | collective-permute-start | bytes 4386824 | tf_op jit(solution)/shard_map/ppermute | solution.py:11
  86.0 2.6 %copy-start.2 = (f32[4,4,3,136,128]{4,3,2,0,1:T(8,128)S(1)}, f32[4,4,3,136,128]{4,3,2,0,1:T(8,128)}, u32[]{:S(2)}) copy-start(f32[4,4,3,136,128]{4,3,2,0,1:T(8,128)} %get-tuple-element.785) | copy-start | bytes 10027012
  95.0 114.9 %collective-permute-start.1 = (f32[7,3,136,128]{3,2,1,0:T(8,128)}, f32[7,3,136,128]{3,2,1,0:T(8,128)}, u32[]{:S(2)}, u32[]{:S(2)}) collective-permute-start(f32[7,3,136,128]{3,2,1,0:T(8,128)} %fusion.47), channel_id=1, source_target_pairs={{0,63},{1,0},{2,1},{3,2},{4,3},{5,4},{6,5},{7,6},{8,7},{9,8},{10,9... | collective-permute-start | bytes 4386824 | tf_op jit(solution)/shard_map/ppermute | solution.py:11
  127.2 2.6 %copy-start.3 = (f32[4,4,3,136,128]{4,3,2,0,1:T(8,128)S(1)}, f32[4,4,3,136,128]{4,3,2,0,1:T(8,128)}, u32[]{:S(2)}) copy-start(f32[4,4,3,136,128]{4,3,2,0,1:T(8,128)} %get-tuple-element.786) | copy-start | bytes 10027012
  136.2 73.8 %collective-permute-start.2 = (f32[7,3,136,128]{3,2,1,0:T(8,128)}, f32[7,3,136,128]{3,2,1,0:T(8,128)}, u32[]{:S(2)}, u32[]{:S(2)}) collective-permute-start(f32[7,3,136,128]{3,2,1,0:T(8,128)} %fusion.45), channel_id=1, source_target_pairs={{0,1},{1,2},{2,3},{3,4},{4,5},{5,6},{6,7},{7,8},{8,9},{9,10},{10,1... | collective-permute-start | bytes 4386824 | tf_op jit(solution)/shard_map/ppermute | solution.py:11
  166.1 2.6 %copy-start.5 = (f32[4,4,3,136,128]{4,3,2,1,0:T(8,128)S(1)}, f32[4,4,3,136,128]{4,3,2,1,0:T(8,128)}, u32[]{:S(2)}) copy-start(f32[4,4,3,136,128]{4,3,2,1,0:T(8,128)} %get-tuple-element.787) | copy-start | bytes 10027012
  175.1 38.4 %collective-permute-start.3 = (f32[7,3,136,128]{3,2,1,0:T(8,128)}, f32[7,3,136,128]{3,2,1,0:T(8,128)}, u32[]{:S(2)}, u32[]{:S(2)}) collective-permute-start(f32[7,3,136,128]{3,2,1,0:T(8,128)} %fusion.40), channel_id=1, source_target_pairs={{0,2},{1,3},{2,4},{3,5},{4,6},{5,7},{6,8},{7,9},{8,10},{9,11},{10,... | collective-permute-start | bytes 4386824 | tf_op jit(solution)/shard_map/ppermute | solution.py:11
  207.2 2.2 copy-start.4
  209.9 11.8 %copy-start.8 = (s32[5]{0:T(128)S(1)}, s32[5]{0:T(128)}, u32[]{:S(2)}) copy-start(s32[5]{0:T(128)} %constant.1777.clone.1) | copy-start | bytes 64
  216.6 9.5 %collective-permute-start.4 = (f32[2,3,136,128]{3,2,1,0:T(8,128)S(1)}, f32[2,3,136,128]{3,2,1,0:T(8,128)S(1)}, u32[]{:S(2)}, u32[]{:S(2)}) collective-permute-start(f32[2,3,136,128]{3,2,1,0:T(8,128)S(1)} %slice.996), channel_id=1, source_target_pairs={{0,64},{64,128},{128,192},{1,65},{65,129},{129,193},{2,66},{66,130... | collective-permute-start | bytes 1253384 | tf_op jit(solution)/shard_map/ppermute | solution.py:17
  222.5 7.1 %collective-permute-start.5 = (f32[1,3,136,128]{3,2,1,0:T(8,128)S(1)}, f32[1,3,136,128]{3,2,1,0:T(8,128)S(1)}, u32[]{:S(2)}, u32[]{:S(2)}) collective-permute-start(f32[1,3,136,128]{3,2,1,0:T(8,128)S(1)} %slice.998), channel_id=1, source_target_pairs={{64,0},{128,64},{192,128},{65,1},{129,65},{193,129},{66,2},{130,66... | collective-permute-start | bytes 626696 | tf_op jit(solution)/shard_map/ppermute | solution.py:17
  229.7 2.4 copy-start.7
  231.1 0.9 copy-start.6
where the time goes:
time: 241 us; the launch traced here: 239 us
  loops' own time  102 us (42%)
  other arithmetic  61.2 us (25%)
  local copies, waits for them, and re-layouts  43.8 us (18%)
  starting transfers between devices  20.3 us (8%)
  waiting for transfers between devices  8.51 us (4%)
    another operation x5, loops' own time, tile_terms(): summed = lax.map(one_row, (padded_values, padded_pairs, offsets))  102 us
    scatter-add x15, other arithmetic, tile_terms(): extended = extended.at[a:a + row_count].add(summed[:, a])  26.2 us
    dynamic_update_slice x20, other arithmetic, tile_terms(): summed = lax.map(one_row, (padded_values, padded_pairs, offsets))  22.3 us
    ppermute x4, starting transfers between devices, passed_along(): lax.ppermute(x, axis, [(i, (i + by) % devices) for i in range(devices)])  13.7 us
    dynamic_slice x20, local copies, waits for them, and re-layouts, tile_terms(): summed = lax.map(one_row, (padded_values, padded_pairs, offsets))  12.5 us
    another operation x5, local copies, waits for them, and re-layouts  8.38 us
    add x5, local copies, waits for them, and re-layouts, tile_terms(): extended = extended.at[a:a + row_count].add(summed[:, a])  6.77 us
    ppermute x2, starting transfers between devices, shifted(): return lax.ppermute(x, axis, pairs)  6.58 us
  transfers between devices with their start and end apart: 6, of which 3 were waited for; matrix products, arithmetic and copies ran while one was open for 30% of the time, Pallas kernels for 0%

commit v1 on v0

v1 whole, which is shorter than its diff:
```python
import jax
import jax.numpy as jnp
from jax import lax
from jax.experimental import pallas as pl
from jax.experimental.pallas import tpu as pltpu
from jax.sharding import PartitionSpec as P

MESH = pl.DeviceIdType.MESH
ORDER = [(3, 0), (2, 0), (3, 1), (2, 1), (3, 2), (2, 2), (0, 0), (0, 1), (0, 2), (1, 0), (1, 1), (1, 2)]
HEAD = 6


def cubic(f):
    p, m1, m2 = f + 1.0, f - 1.0, f - 2.0
    sixth = 1.0 / 6.0
    return (-f * m1 * m2 * sixth, p * m1 * m2 * 0.5, -p * f * m2 * 0.5, p * f * m1 * sixth)


def kernel(
    tile_ref, col_ref, x_hbm, fx_ref, fy_ref, inv_ref, cpl_ref, out_ref,
    own, left, right, acc, from_prev, from_next, fxl, fxr, fyl, fyr,
    edge_r, edge_l, hop_l, hop_r, far_l, far_r, weights, ahi, alo, bcol,
    own_sem, send_sem, recv_sem, fsend, frecv, esend, erecv, lsend, lrecv,
):
    rows, tracers, levels, cols = x_hbm.shape
    half = levels // 2
    nlon, nlat = lax.axis_size("lon"), lax.axis_size("lat")
    lon, lat = lax.axis_index("lon"), lax.axis_index("lat")
    to_right = (lat, lax.rem(lon + 1, nlon))
    to_left = (lat, lax.rem(lon + nlon - 1, nlon))
    has_prev, has_next = lat > 0, lat < nlat - 1

    barrier = pltpu.get_barrier_semaphore()
    pl.semaphore_signal(barrier, inc=1, device_id=to_right, device_id_type=MESH)
    pl.semaphore_signal(barrier, inc=1, device_id=to_left, device_id_type=MESH)

    @pl.when(has_prev)
    def _():
        pl.semaphore_signal(barrier, inc=1, device_id=(lat - 1, lon), device_id_type=MESH)

    @pl.when(has_next)
    def _():
        pl.semaphore_signal(barrier, inc=1, device_id=(lat + 1, lon), device_id_type=MESH)

    own_copy = pltpu.make_async_copy(x_hbm, own, own_sem)
    own_copy.start()

    def remote(src, dst, ss, rs, to):
        return pltpu.make_async_remote_copy(src, dst, ss, rs, device_id=to, device_id_type=MESH)

    pl.semaphore_wait(barrier, 2 + has_prev.astype(jnp.int32) + has_next.astype(jnp.int32))

    small = [
        remote(fx_ref, fxl, fsend.at[0], frecv.at[0], to_right),
        remote(fy_ref, fyl, fsend.at[1], frecv.at[1], to_right),
        remote(fx_ref, fxr, fsend.at[2], frecv.at[2], to_left),
        remote(fy_ref, fyr, fsend.at[3], frecv.at[3], to_left),
    ]
    for copy in small:
        copy.start()
    big = []
    for k, (r, t) in enumerate(ORDER):
        big.append((
            remote(x_hbm.at[r, t], left.at[k], send_sem.at[0, k], recv_sem.at[0, k], to_right),
            remote(x_hbm.at[r, t], right.at[k], send_sem.at[1, k], recv_sem.at[1, k], to_left),
        ))
    for a, b in big[:HEAD]:
        a.start()
        b.start()

    own_copy.wait()
    eye = lax.broadcasted_iota(jnp.int32, (cols, cols), 0) == lax.broadcasted_iota(jnp.int32, (cols, cols), 1)
    rest = levels - cols
    eye_rest = lax.broadcasted_iota(jnp.int32, (rest, cols), 0) == lax.broadcasted_iota(jnp.int32, (rest, cols), 1)
    for r in range(rows):
        for t in range(tracers):
            k = r * tracers + t
            for lane, edge in ((cols - 1, edge_r), (0, edge_l)):
                column = jnp.broadcast_to(own[r, t, :, lane : lane + 1], (levels, cols))
                edge[k : k + 1, 0:cols] = jnp.sum(jnp.where(eye, column[:cols], 0.0), axis=0, keepdims=True)
                edge[k : k + 1, cols : 2 * cols] = jnp.sum(jnp.where(eye_rest, column[cols:], 0.0), axis=0, keepdims=True)
    base = rows * tracers
    for lane, edge in ((cols - 1, edge_r), (0, edge_l)):
        edge[base : base + rows, 0:cols] = jnp.broadcast_to(fx_ref[:, lane : lane + 1], (rows, cols))
        edge[base : base + rows, cols : 2 * cols] = jnp.broadcast_to(fy_ref[:, lane : lane + 1], (rows, cols))

    sub = lax.broadcasted_iota(jnp.int32, (levels, cols), 0)
    for r in range(rows):
        top = jnp.concatenate([inv_ref[r, 0], jnp.zeros((half, half), jnp.float32)], axis=1)
        low = jnp.concatenate([jnp.zeros((half, half), jnp.float32), inv_ref[r, 1]], axis=1)
        whole = jnp.concatenate([top, low], axis=0)
        hi = whole.astype(jnp.bfloat16)
        ahi[r] = hi
        alo[r] = (whole - hi.astype(jnp.float32)).astype(jnp.bfloat16)
        column = jnp.concatenate([inv_ref[r, 0, :, half - 1 : half], inv_ref[r, 1, :, 0:1]], axis=0)
        bcol[r] = jnp.broadcast_to(column, (levels, cols))

    edge_copies = [
        remote(edge_r, hop_l, esend.at[0], erecv.at[0], to_right),
        remote(edge_l, hop_r, esend.at[1], erecv.at[1], to_left),
        remote(hop_l, far_l, esend.at[2], erecv.at[2], to_right),
        remote(hop_r, far_r, esend.at[3], erecv.at[3], to_left),
    ]
    edge_copies[0].start()
    edge_copies[1].start()
    edge_copies[0].wait_recv()
    edge_copies[2].start()
    edge_copies[1].wait_recv()
    edge_copies[3].start()
    for a, b in big[HEAD:]:
        a.start()
        b.start()

    for copy in small:
        copy.wait_recv()
    edge_copies[2].wait_recv()
    edge_copies[3].wait_recv()

    lane = lax.broadcasted_iota(jnp.int32, (8, cols), 1)
    shifts = [tile_ref[r] * cols + col_ref[r] for r in range(rows)]

    def sources(s, b):
        d = s + (b - 1)
        return lax.shift_right_arithmetic(lane + d, 7), jnp.bitwise_and(d, cols - 1)

    def vec(ref, r, c0=0):
        return jnp.broadcast_to(ref[r : r + 1, c0 : c0 + cols], (8, cols))

    for r in range(rows):
        s = shifts[r]
        fx3 = (vec(fx_ref, r), vec(fxl, r), vec(fxr, r))
        fy3 = (vec(fy_ref, r), vec(fyl, r), vec(fyr, r))
        for b in range(4):
            where, turn = sources(s, b)
            shifted = []
            for (here, l, rt), c0 in ((fx3, 0), (fy3, cols)):
                v = jnp.where(where > 0, l, jnp.where(where < 0, rt, here))
                if b == 3:
                    v = jnp.where(where == 2, vec(far_l, base + r, c0), v)
                if b == 0:
                    v = jnp.where(where == -2, vec(far_r, base + r, c0), v)
                shifted.append(pltpu.roll(v, turn, 1))
            wx = cubic(shifted[0])[b]
            for a, wy in enumerate(cubic(shifted[1])):
                weights[r, a * 4 + b] = wx * wy

    lane8 = lane - lax.broadcasted_iota(jnp.int32, (8, cols), 0)

    def spread(k, r, t):
        s = shifts[r]
        sv = jnp.full((8, cols), 0, jnp.int32) + s
        lo_right, hi_left = sv <= 0, sv >= -1
        src = [sources(s, b) for b in range(4)]
        g = [[weights[r, a * 4 + b] for b in range(4)] for a in range(4)]
        kk = r * tracers + t
        for i in range(levels // 8):
            rs = slice(8 * i, 8 * i + 8)
            here, l, rt = own[r, t, rs, :], left[k, rs, :], right[k, rs, :]
            c0 = cols * ((8 * i) // cols)
            far = jnp.where(hi_left, vec(far_l, kk, c0), vec(far_r, kk, c0))
            far = jnp.sum(jnp.where(lane8 == (8 * i) % cols, far, 0.0), axis=1, keepdims=True)
            far = jnp.broadcast_to(far, (8, cols))
            near_lo, near_hi = jnp.where(lo_right, rt, l), jnp.where(hi_left, l, rt)
            u = []
            for b in range(4):
                where, turn = src[b]
                v = jnp.where(where == 0, here, near_lo if b < 2 else near_hi)
                if b == 3:
                    v = jnp.where(where == 2, far, v)
                if b == 0:
                    v = jnp.where(where == -2, far, v)
                u.append(pltpu.roll(v, turn, 1))
            for a in range(4):
                part = (g[a][0] * u[0] + g[a][1] * u[1]) + (g[a][2] * u[2] + g[a][3] * u[3])
                first = r == 3 or (r == 2 and a == 0) or (r == 0 and a < 2)
                acc[t, r + a, rs, :] = part if first else acc[t, r + a, rs, :] + part

    def next_copy(t):
        return remote(acc.at[t, pl.ds(rows + 1, 2)], from_prev.at[t], lsend.at[0, t], lrecv.at[0, t], (lat + 1, lon))

    def prev_copy(t):
        return remote(acc.at[t, 0], from_next.at[t], lsend.at[1, t], lrecv.at[1, t], (lat - 1, lon))

    def final(t):
        @pl.when(has_prev)
        def _():
            next_copy(t).wait_recv()

        @pl.when(has_next)
        def _():
            prev_copy(t).wait_recv()

        for i in range(rows):
            x = acc[t, i + 1]
            if i < 2:
                x = x + from_prev[t, i]
            if i == rows - 1:
                x = x + from_next[t]
            hi = x.astype(jnp.bfloat16)
            lo = (x - hi.astype(jnp.float32)).astype(jnp.bfloat16)
            p = jnp.dot(ahi[i], hi, preferred_element_type=jnp.float32)
            p = p + jnp.dot(ahi[i], lo, preferred_element_type=jnp.float32)
            p = p + jnp.dot(alo[i], hi, preferred_element_type=jnp.float32)
            c = cpl_ref[i : i + 1, :]
            above = jnp.broadcast_to(c * p[half : half + 1], (levels, cols))
            below = jnp.broadcast_to(c * p[half - 1 : half], (levels, cols))
            out_ref[i, t] = p + bcol[i] * jnp.where(sub < half, above, below)

    @pl.when(jnp.logical_not(has_prev))
    def _():
        from_prev[...] = jnp.zeros_like(from_prev)

    @pl.when(jnp.logical_not(has_next))
    def _():
        from_next[...] = jnp.zeros_like(from_next)

    due = []
    for k, (r, t) in enumerate(ORDER):
        big[k][0].wait_recv()
        big[k][1].wait_recv()
        spread(k, r, t)
        for send in due:
            send()
        due = []
        if r == 2:
            def send(t=t):
                @pl.when(has_next)
                def _():
                    next_copy(t).start()
            due.append(send)
        if r == 0:
            def send(t=t):
                @pl.when(has_prev)
                def _():
                    prev_copy(t).start()
            due.append(send)
        if r == 1:
            final(t)

    for copy in small + edge_copies:
        copy.wait_send()
    for a, b in big:
        a.wait_send()
        b.wait_send()

    @pl.when(has_next)
    def _():
        for t in range(tracers):
            next_copy(t).wait_send()

    @pl.when(has_prev)
    def _():
        for t in range(tracers):
            prev_copy(t).wait_send()


def on_device(adjoint_in, frac_x, frac_y, dep_tile, dep_col, block_inverse, coupling):
    rows, tracers, levels, cols = adjoint_in.shape
    blocks = rows * tracers
    f32, dma = jnp.float32, pltpu.SemaphoreType.DMA
    vmem, smem = pl.BlockSpec(memory_space=pltpu.VMEM), pl.BlockSpec(memory_space=pltpu.SMEM)
    return pl.pallas_call(
        kernel,
        out_shape=jax.ShapeDtypeStruct(adjoint_in.shape, f32),
        in_specs=[smem, smem, pl.BlockSpec(memory_space=pl.ANY), vmem, vmem, vmem, vmem],
        out_specs=vmem,
        scratch_shapes=[
            pltpu.VMEM((rows, tracers, levels, cols), f32),
            pltpu.VMEM((blocks, levels, cols), f32),
            pltpu.VMEM((blocks, levels, cols), f32),
            pltpu.VMEM((tracers, rows + 3, levels, cols), f32),
            pltpu.VMEM((tracers, 2, levels, cols), f32),
            pltpu.VMEM((tracers, levels, cols), f32),
            *[pltpu.VMEM((rows, cols), f32)] * 4,
            *[pltpu.VMEM((blocks + rows, 2 * cols), f32)] * 6,
            pltpu.VMEM((rows, 16, 8, cols), f32),
            pltpu.VMEM((rows, levels, levels), jnp.bfloat16),
            pltpu.VMEM((rows, levels, levels), jnp.bfloat16),
            pltpu.VMEM((rows, levels, cols), f32),
            dma,
            dma((2, blocks)),
            dma((2, blocks)),
            dma((4,)),
            dma((4,)),
            dma((4,)),
            dma((4,)),
            dma((2, tracers)),
            dma((2, tracers)),
        ],
        compiler_params=pltpu.CompilerParams(collective_id=0, has_side_effects=True),
    )(dep_tile, dep_col, adjoint_in, frac_x, frac_y, block_inverse, coupling)


def solution(mesh):
    return jax.shard_map(
        on_device,
        mesh=mesh,
        in_specs=(
            P("lat", None, None, "lon"),
            P("lat", "lon"),
            P("lat", "lon"),
            P("lat"),
            P("lat"),
            P("lat", None, None, None),
            P("lat", "lon"),
        ),
        out_specs=P("lat", None, None, "lon"),
        check_vma=False,
    )
```

time: 241 us -> 47.7 us (0.20)
  loops' own time: 102 us -> 0 us
  other arithmetic: 61.2 us -> 0 us
  Pallas kernels: 0 us -> 43.7 us
  local copies, waits for them, and re-layouts: 43.8 us -> 3.79 us
  starting transfers between devices: 20.3 us -> 0 us
  waiting for transfers between devices: 8.51 us -> 0 us
    another operation x5 -> x0, loops' own time: 102 us -> none  [tile_terms(): summed = lax.map(one_row, (padded_values, padded_pairs, offsets))]
    pallas_call x0 -> x1, Pallas kernels: none -> 43.7 us  [on_device(): pl.pallas_call(kernel, out_shape=jax.ShapeDtypeStruct(adjoint_in.shape, f...]
    scatter-add x17 -> x0, other arithmetic: 26.3 us -> none  [the longest x15 26.2 us: tile_terms(): extended = extended.at[a:a + row_count].add(summed[:, a])]
    dynamic_update_slice x20 -> x0, other arithmetic: 22.3 us -> none  [tile_terms(): summed = lax.map(one_row, (padded_values, padded_pairs, offsets))]
    ppermute x6 -> x0, starting transfers between devices: 20.3 us -> none  [the longest x4 13.7 us: passed_along(): lax.ppermute(x, axis, [(i, (i + by) % devices) for i in range(devices)])]
    dynamic_slice x20 -> x0, local copies, waits for them, and re-layouts: 12.5 us -> none  [tile_terms(): summed = lax.map(one_row, (padded_values, padded_pairs, offsets))]
    ppermute x6 -> x0, waiting for transfers between devices: 8.51 us -> none  [the longest x2 4.97 us: shifted(): return lax.ppermute(x, axis, pairs)]
    another operation x5 -> x0, local copies, waits for them, and re-layouts: 8.38 us -> none
  transfers between devices with their start and end apart: 6 -> 0, of which waited for: 3 -> 0; matrix products, arithmetic and copies ran while one was open for 30% -> 0% of each run, Pallas kernels for 0% -> 0%
where the time goes in v1:
time: 47.7 us; the launch traced here: 47.5 us
  Pallas kernels  43.7 us (92%)
  local copies, waits for them, and re-layouts  3.79 us (8%)
    pallas_call x1, Pallas kernels, on_device(): pl.pallas_call(kernel, out_shape=jax.ShapeDtypeStruct(adjoint_in.shape, f...  43.7 us
    unnamed x2, local copies, waits for them, and re-layouts  3.79 us

profile of v1, /device:TPU:1, one launch (start us, length us, event | category | flops | bytes accessed | tf_op | source)
XLA Modules:
  0.0 47.5 jit_solution(3875613080570817913)
XLA Ops:
  0.0 1.7 %copy.8.inv_ref = f32[4,2,68,68]{3,2,1,0:T(8,128)} copy(f32[4,2,68,68]{3,1,2,0:T(2,128)} %param.12) | data formatting | bytes 295936 | tf_op args[5]
  1.7 43.7 %shard_map.73 = f32[4,3,136,128]{3,2,1,0:T(8,128)} custom-call(s32[4]{0:T(128)} %tile_ref.1, s32[4]{0:T(128)} %col_ref.1, f32[4,3,136,128]{3,2,1,0:T(8,128)} %x_hbm.1, f32[4,128]{1,0:T(4,128)} %fx_ref.1, f32[4,128]{1,0:T(4,128)} %fy_ref.1, f32[4,2,68,68]{3,2,1,0:T(8,128)} %copy.8.inv_ref, f32[4,128]{1,0:T(4,128)} %cpl_ref.1), custom_call_target="tpu_custom_call" | custom-call | tf_op jit(solution)/shard_map/pallas_call | solution.py:262
  45.4 2.1 %copy.10 = f32[4,3,136,128]{3,2,1,0:T(8,128)} copy(f32[4,3,136,128]{3,2,1,0:T(8,128)} %shard_map.73) | data formatting | bytes 1671168

commit v2 on v1

--- a/solution.py
+++ b/solution.py
@@ -7,7 +7,7 @@
 
 MESH = pl.DeviceIdType.MESH
 ORDER = [(3, 0), (2, 0), (3, 1), (2, 1), (3, 2), (2, 2), (0, 0), (0, 1), (0, 2), (1, 0), (1, 1), (1, 2)]
-HEAD = 6
+HEAD, HEAD2 = 2, 4
 
 
 def cubic(f):
@@ -17,10 +17,10 @@
 
 
 def kernel(
-    tile_ref, col_ref, x_hbm, fx_ref, fy_ref, inv_ref, cpl_ref, out_ref,
-    own, left, right, acc, from_prev, from_next, fxl, fxr, fyl, fyr,
+    tile_hbm, col_hbm, x_hbm, fx_hbm, fy_hbm, inv_hbm, cpl_hbm, out_ref,
+    tile_ref, col_ref, fx_ref, fy_ref, inv_ref, cpl_ref, own, left, right, acc, from_prev, from_next, fxl, fxr, fyl, fyr,
     edge_r, edge_l, hop_l, hop_r, far_l, far_r, weights, ahi, alo, bcol,
-    own_sem, send_sem, recv_sem, fsend, frecv, esend, erecv, lsend, lrecv,
+    own_sem, in_sem, send_sem, recv_sem, fsend, frecv, esend, erecv, lsend, lrecv,
 ):
     rows, tracers, levels, cols = x_hbm.shape
     half = levels // 2
@@ -42,22 +42,23 @@
     def _():
         pl.semaphore_signal(barrier, inc=1, device_id=(lat + 1, lon), device_id_type=MESH)
 
-    own_copy = pltpu.make_async_copy(x_hbm, own, own_sem)
-    own_copy.start()
-
     def remote(src, dst, ss, rs, to):
         return pltpu.make_async_remote_copy(src, dst, ss, rs, device_id=to, device_id_type=MESH)
 
     pl.semaphore_wait(barrier, 2 + has_prev.astype(jnp.int32) + has_next.astype(jnp.int32))
 
+    edge_copies = [
+        remote(edge_r, hop_l, esend.at[0], erecv.at[0], to_right),
+        remote(edge_l, hop_r, esend.at[1], erecv.at[1], to_left),
+        remote(hop_l, far_l, esend.at[2], erecv.at[2], to_right),
+        remote(hop_r, far_r, esend.at[3], erecv.at[3], to_left),
+    ]
     small = [
-        remote(fx_ref, fxl, fsend.at[0], frecv.at[0], to_right),
-        remote(fy_ref, fyl, fsend.at[1], frecv.at[1], to_right),
-        remote(fx_ref, fxr, fsend.at[2], frecv.at[2], to_left),
-        remote(fy_ref, fyr, fsend.at[3], frecv.at[3], to_left),
+        remote(fx_hbm, fxl, fsend.at[0], frecv.at[0], to_right),
+        remote(fy_hbm, fyl, fsend.at[1], frecv.at[1], to_right),
+        remote(fx_hbm, fxr, fsend.at[2], frecv.at[2], to_left),
+        remote(fy_hbm, fyr, fsend.at[3], frecv.at[3], to_left),
     ]
-    for copy in small:
-        copy.start()
     big = []
     for k, (r, t) in enumerate(ORDER):
         big.append((
@@ -67,6 +68,21 @@
     for a, b in big[:HEAD]:
         a.start()
         b.start()
+    for copy in small:
+        copy.start()
+    own_copy = pltpu.make_async_copy(x_hbm, own, own_sem)
+    own_copy.start()
+    loads = [
+        pltpu.make_async_copy(src, dst, in_sem.at[i])
+        for i, (src, dst) in enumerate((
+            (fx_hbm, fx_ref), (fy_hbm, fy_ref), (tile_hbm, tile_ref),
+            (col_hbm, col_ref), (cpl_hbm, cpl_ref), (inv_hbm, inv_ref),
+        ))
+    ]
+    for copy in loads:
+        copy.start()
+    for copy in loads[:2]:
+        copy.wait()
 
     own_copy.wait()
     eye = lax.broadcasted_iota(jnp.int32, (cols, cols), 0) == lax.broadcasted_iota(jnp.int32, (cols, cols), 1)
@@ -84,32 +100,32 @@
         edge[base : base + rows, 0:cols] = jnp.broadcast_to(fx_ref[:, lane : lane + 1], (rows, cols))
         edge[base : base + rows, cols : 2 * cols] = jnp.broadcast_to(fy_ref[:, lane : lane + 1], (rows, cols))
 
+    edge_copies[0].start()
+    edge_copies[1].start()
+    for a, b in big[HEAD:HEAD2]:
+        a.start()
+        b.start()
+    for copy in loads[2:]:
+        copy.wait()
+
+    edge_copies[0].wait_recv()
+    edge_copies[2].start()
+    edge_copies[1].wait_recv()
+    edge_copies[3].start()
+    for a, b in big[HEAD2:]:
+        a.start()
+        b.start()
+
     sub = lax.broadcasted_iota(jnp.int32, (levels, cols), 0)
     for r in range(rows):
-        top = jnp.concatenate([inv_ref[r, 0], jnp.zeros((half, half), jnp.float32)], axis=1)
-        low = jnp.concatenate([jnp.zeros((half, half), jnp.float32), inv_ref[r, 1]], axis=1)
+        top = jnp.concatenate([inv_ref[r, :, 0, :], jnp.zeros((half, half), jnp.float32)], axis=1)
+        low = jnp.concatenate([jnp.zeros((half, half), jnp.float32), inv_ref[r, :, 1, :]], axis=1)
         whole = jnp.concatenate([top, low], axis=0)
         hi = whole.astype(jnp.bfloat16)
         ahi[r] = hi
         alo[r] = (whole - hi.astype(jnp.float32)).astype(jnp.bfloat16)
-        column = jnp.concatenate([inv_ref[r, 0, :, half - 1 : half], inv_ref[r, 1, :, 0:1]], axis=0)
+        column = jnp.concatenate([inv_ref[r, :, 0, half - 1 : half], inv_ref[r, :, 1, 0:1]], axis=0)
         bcol[r] = jnp.broadcast_to(column, (levels, cols))
-
-    edge_copies = [
-        remote(edge_r, hop_l, esend.at[0], erecv.at[0], to_right),
-        remote(edge_l, hop_r, esend.at[1], erecv.at[1], to_left),
-        remote(hop_l, far_l, esend.at[2], erecv.at[2], to_right),
-        remote(hop_r, far_r, esend.at[3], erecv.at[3], to_left),
-    ]
-    edge_copies[0].start()
-    edge_copies[1].start()
-    edge_copies[0].wait_recv()
-    edge_copies[2].start()
-    edge_copies[1].wait_recv()
-    edge_copies[3].start()
-    for a, b in big[HEAD:]:
-        a.start()
-        b.start()
 
     for copy in small:
         copy.wait_recv()
@@ -214,26 +230,20 @@
     def _():
         from_next[...] = jnp.zeros_like(from_next)
 
-    due = []
     for k, (r, t) in enumerate(ORDER):
         big[k][0].wait_recv()
         big[k][1].wait_recv()
         spread(k, r, t)
-        for send in due:
-            send()
-        due = []
         if r == 2:
-            def send(t=t):
-                @pl.when(has_next)
-                def _():
-                    next_copy(t).start()
-            due.append(send)
+            @pl.when(has_next)
+            def _(t=t):
+                next_copy(t).start()
+
         if r == 0:
-            def send(t=t):
-                @pl.when(has_prev)
-                def _():
-                    prev_copy(t).start()
-            due.append(send)
+            @pl.when(has_prev)
+            def _(t=t):
+                prev_copy(t).start()
+
         if r == 1:
             final(t)
 
@@ -258,13 +268,18 @@
     rows, tracers, levels, cols = adjoint_in.shape
     blocks = rows * tracers
     f32, dma = jnp.float32, pltpu.SemaphoreType.DMA
-    vmem, smem = pl.BlockSpec(memory_space=pltpu.VMEM), pl.BlockSpec(memory_space=pltpu.SMEM)
     return pl.pallas_call(
         kernel,
-        out_shape=jax.ShapeDtypeStruct(adjoint_in.shape, f32),
-        in_specs=[smem, smem, pl.BlockSpec(memory_space=pl.ANY), vmem, vmem, vmem, vmem],
-        out_specs=vmem,
+        out_shape=pltpu.VMEM(adjoint_in.shape, f32),
+        in_specs=[pl.BlockSpec(memory_space=pl.ANY)] * 7,
+        out_specs=pl.BlockSpec(memory_space=pltpu.VMEM),
         scratch_shapes=[
+            pltpu.SMEM(dep_tile.shape, jnp.int32),
+            pltpu.SMEM(dep_col.shape, jnp.int32),
+            pltpu.VMEM((rows, cols), f32),
+            pltpu.VMEM((rows, cols), f32),
+            pltpu.VMEM((rows, levels // 2, 2, levels // 2), f32),
+            pltpu.VMEM((rows, cols), f32),
             pltpu.VMEM((rows, tracers, levels, cols), f32),
             pltpu.VMEM((blocks, levels, cols), f32),
             pltpu.VMEM((blocks, levels, cols), f32),
@@ -278,6 +293,7 @@
             pltpu.VMEM((rows, levels, levels), jnp.bfloat16),
             pltpu.VMEM((rows, levels, cols), f32),
             dma,
+            dma((6,)),
             dma((2, blocks)),
             dma((2, blocks)),
             dma((4,)),
@@ -288,7 +304,7 @@
             dma((2, tracers)),
         ],
         compiler_params=pltpu.CompilerParams(collective_id=0, has_side_effects=True),
-    )(dep_tile, dep_col, adjoint_in, frac_x, frac_y, block_inverse, coupling)
+    )(dep_tile, dep_col, adjoint_in, frac_x, frac_y, jnp.swapaxes(block_inverse, 1, 2), coupling)
 
 
 def solution(mesh):

time: 47.7 us -> 39.4 us (0.83)
  Pallas kernels: 43.7 us -> 38.4 us
  local copies, waits for them, and re-layouts: 3.79 us -> 0.9 us
    pallas_call x1, Pallas kernels: 43.7 us -> 38.4 us  [on_device(): pl.pallas_call(kernel, out_shape=pltpu.VMEM(adjoint_in.shape, f32), in_sp...]
    unnamed x2 -> x1, local copies, waits for them, and re-layouts: 3.79 us -> 0.9 us
where the time goes in v2:
time: 39.4 us
  Pallas kernels  38.4 us (97%)
  local copies, waits for them, and re-layouts  0.9 us (2%)
    pallas_call x1, Pallas kernels, on_device(): pl.pallas_call(kernel, out_shape=pltpu.VMEM(adjoint_in.shape, f32), in_sp...  38.4 us
    unnamed x1, local copies, waits for them, and re-layouts  0.9 us

profile of v2, /device:TPU:1, one launch (start us, length us, event | category | flops | bytes accessed | tf_op | source)
XLA Modules:
  0.0 39.4 jit_solution(8442665544789122709)
XLA Ops:
  0.0 38.4 %shard_map.73 = f32[4,3,136,128]{3,2,1,0:T(8,128)S(1)} custom-call(s32[4]{0:T(128)} %tile_hbm.1, s32[4]{0:T(128)} %col_hbm.1, f32[4,3,136,128]{3,2,1,0:T(8,128)} %x_hbm.1, f32[4,128]{1,0:T(4,128)} %fx_hbm.1, f32[4,128]{1,0:T(4,128)} %fy_hbm.1, f32[4,68,2,68]{3,2,1,0:T(2,128)} %bitcast.1, f32[4,128]{1,0:T(4,128)} %cpl_hbm.1), custom_call_target="tpu_custom_call" | custom-call | tf_op jit(solution)/shard_map/pallas_call | solution.py:271
  38.5 0.9 %copy.9 = f32[4,3,136,128]{3,2,1,0:T(8,128)} copy(f32[4,3,136,128]{3,2,1,0:T(8,128)S(1)} %shard_map.73) | data formatting | bytes 1671168

commit v3 on v2

--- a/solution.py
+++ b/solution.py
@@ -110,10 +110,11 @@
 
     edge_copies[0].wait_recv()
     edge_copies[2].start()
+    for a, _ in big[HEAD2:]:
+        a.start()
     edge_copies[1].wait_recv()
     edge_copies[3].start()
-    for a, b in big[HEAD2:]:
-        a.start()
+    for _, b in big[HEAD2:]:
         b.start()
 
     sub = lax.broadcasted_iota(jnp.int32, (levels, cols), 0)

time: 39.4 us -> 35.9 us (0.911)
  Pallas kernels: 38.4 us -> 34.9 us
    pallas_call x1, Pallas kernels: 38.4 us -> 34.9 us  [on_device(): pl.pallas_call(kernel, out_shape=pltpu.VMEM(adjoint_in.shape, f32), in_sp...]
where the time goes in v3:
time: 35.9 us; the launch traced here: 35.8 us
  Pallas kernels  34.9 us (97%)
  local copies, waits for them, and re-layouts  0.9 us (3%)
    pallas_call x1, Pallas kernels, on_device(): pl.pallas_call(kernel, out_shape=pltpu.VMEM(adjoint_in.shape, f32), in_sp...  34.9 us
    unnamed x1, local copies, waits for them, and re-layouts  0.9 us

profile of v3, /device:TPU:1, one launch (start us, length us, event | category | flops | bytes accessed | tf_op | source)
XLA Modules:
  0.0 35.8 jit_solution(16541129969797885359)
XLA Ops:
  0.0 34.9 %shard_map.73 = f32[4,3,136,128]{3,2,1,0:T(8,128)S(1)} custom-call(s32[4]{0:T(128)} %tile_hbm.1, s32[4]{0:T(128)} %col_hbm.1, f32[4,3,136,128]{3,2,1,0:T(8,128)} %x_hbm.1, f32[4,128]{1,0:T(4,128)} %fx_hbm.1, f32[4,128]{1,0:T(4,128)} %fy_hbm.1, f32[4,68,2,68]{3,2,1,0:T(2,128)} %bitcast.1, f32[4,128]{1,0:T(4,128)} %cpl_hbm.1), custom_call_target="tpu_custom_call" | custom-call | tf_op jit(solution)/shard_map/pallas_call | solution.py:272
  34.9 0.9 %copy.9 = f32[4,3,136,128]{3,2,1,0:T(8,128)} copy(f32[4,3,136,128]{3,2,1,0:T(8,128)S(1)} %shard_map.73) | data formatting | bytes 1671168

commit v4 on v3

--- a/solution.py
+++ b/solution.py
@@ -6,7 +6,7 @@
 from jax.sharding import PartitionSpec as P
 
 MESH = pl.DeviceIdType.MESH
-ORDER = [(3, 0), (2, 0), (3, 1), (2, 1), (3, 2), (2, 2), (0, 0), (0, 1), (0, 2), (1, 0), (1, 1), (1, 2)]
+ORDER = [(0, 0), (0, 1), (0, 2), (3, 0), (2, 0), (3, 1), (2, 1), (3, 2), (2, 2), (1, 0), (1, 1), (1, 2)]
 HEAD, HEAD2 = 2, 4
 
 
@@ -189,7 +189,7 @@
                 u.append(pltpu.roll(v, turn, 1))
             for a in range(4):
                 part = (g[a][0] * u[0] + g[a][1] * u[1]) + (g[a][2] * u[2] + g[a][3] * u[3])
-                first = r == 3 or (r == 2 and a == 0) or (r == 0 and a < 2)
+                first = r == 0 or (r == 3 and a > 0)
                 acc[t, r + a, rs, :] = part if first else acc[t, r + a, rs, :] + part
 
     def next_copy(t):

time: 35.9 us -> 35.9 us (level)
  no operation moved by 1% of the time
where the time goes in v4:
time: 35.9 us; the launch traced here: 35.8 us
  Pallas kernels  34.9 us (97%)
  local copies, waits for them, and re-layouts  0.9 us (3%)
    pallas_call x1, Pallas kernels, on_device(): pl.pallas_call(kernel, out_shape=pltpu.VMEM(adjoint_in.shape, f32), in_sp...  34.9 us
    unnamed x1, local copies, waits for them, and re-layouts  0.9 us

profile of v4, /device:TPU:1, one launch (start us, length us, event | category | flops | bytes accessed | tf_op | source)
XLA Modules:
  0.0 35.8 jit_solution(4268782565491636915)
XLA Ops:
  0.0 34.9 %shard_map.73 = f32[4,3,136,128]{3,2,1,0:T(8,128)S(1)} custom-call(s32[4]{0:T(128)} %tile_hbm.1, s32[4]{0:T(128)} %col_hbm.1, f32[4,3,136,128]{3,2,1,0:T(8,128)} %x_hbm.1, f32[4,128]{1,0:T(4,128)} %fx_hbm.1, f32[4,128]{1,0:T(4,128)} %fy_hbm.1, f32[4,68,2,68]{3,2,1,0:T(2,128)} %bitcast.1, f32[4,128]{1,0:T(4,128)} %cpl_hbm.1), custom_call_target="tpu_custom_call" | custom-call | tf_op jit(solution)/shard_map/pallas_call | solution.py:272
  34.9 0.9 %copy.9 = f32[4,3,136,128]{3,2,1,0:T(8,128)} copy(f32[4,3,136,128]{3,2,1,0:T(8,128)S(1)} %shard_map.73) | data formatting | bytes 1671168
